TPU v7x, 256 devices: a whole 4x4x8 slice. The times are simulated.
256 devices in a mesh: member: 2 (over core), rep: 8 (over z), tensor: 16 (over x, y).
Axes of the slice: x: 4, y: 4, z: 8, core: 2. Of those that a mesh axis runs over, the one named last changes fastest.
Arguments:
- queries: bfloat16 [2, 64, 32, 128], P('member', 'rep'), parts along dimension 1, may hold values from -110 to 110
- keys: bfloat16 [2, 64, 8192, 128], P('member', 'rep', 'tensor'), parts along dimension 1, may hold values from -4.2 to 4.2
- values: bfloat16 [2, 64, 8192, 128], P('member', 'rep', 'tensor'), parts along dimension 1, may hold values from -6 to 6
- lengths: int32 [64], P('rep'), parts along dimension 0, may hold values from 256 to 2048, as said below
- targets: int32 [64], P('rep'), parts along dimension 0, may hold values from 0 to 16383
- residual: bfloat16 [2, 64, 4096], P('member', 'rep'), parts along dimension 1, may hold values from -32 to 32
- out_weight: bfloat16 [2, 4096, 4096], P('member', 'tensor'), may hold values from -0.75 to 0.75
- norm_gain: float32 [2, 4096], P('member'), may hold values from 0.5 to 1.5
- head_weight: bfloat16 [2, 4096, 16384], P('member', None, 'tensor'), may hold values from -0.2 to 0.2878906
Outputs:
- mean_logprobs: float32 [64, 16384], P(('rep', 'member'), 'tensor'), parts along dimension 0
- target_logprob: float32 [64], P(('rep', 'member')), parts along dimension 0
There are 8 independent parts, one for each index of `rep`. A program takes and returns all parts, laid end to end along the dimension named above; an argument that names none is the same for every part. Nothing has to cross between parts.
Inputs may be any that keep to these rules, and one draw needn't show every extreme that they name: `lengths`: some row of every draw has all 2048 slots live.
All inputs are finite; a program needn't handle non-finite values.
Results may differ from a plain program's by a relative error of at most 0.004.
Values may be sent and summed in bfloat16 or wider, within the bound.
A program may use at most 64 MiB of HBM per device.

v0:
```python
import jax
import jax.numpy as jnp
from jax import lax
from jax.sharding import PartitionSpec as P

HEADS = 32
KV_HEADS = 4


def for_sending(shard):

    def short(part):
        return part.astype(jnp.bfloat16) if part.dtype == jnp.float32 else part

    return jax.tree.map(short, shard)


def swapped(block, axis, distance):
    count = lax.axis_size(axis)
    route = []
    for low in range(count):
        high = low | 1 << distance
        if high != low and high < count:
            route += [(low, high), (high, low)]
    return lax.ppermute(block, axis, route)


def join_partial(earlier, later):
    peak_one, total_one, weighted_one = earlier
    peak_two, total_two, weighted_two = later
    peak_new = jnp.maximum(peak_one, peak_two)
    scale_one = jnp.exp(peak_one - peak_new)
    scale_two = jnp.exp(peak_two - peak_new)
    total_new = total_one * scale_one + total_two * scale_two
    weighted_new = weighted_one * scale_one[..., None] + weighted_two * scale_two[..., None]
    return (peak_new, total_new, weighted_new)


def local(queries, keys, values, lengths, targets, residual, out_weight, norm_gain, head_weight):
    axis_width = lax.axis_size("tensor")
    my_rank = lax.axis_index("tensor")
    member_rank = lax.axis_index("member")
    group_size = axis_width // KV_HEADS
    heads_kv = HEADS // KV_HEADS
    heads_dev = HEADS // axis_width
    row_count = keys.shape[1]
    key_span = keys.shape[2]
    head_depth = keys.shape[3]
    kv_index = my_rank // group_size
    slot_first = my_rank % group_size * key_span
    group_query = lax.dynamic_slice_in_dim(queries[0], kv_index * heads_kv, heads_kv, 1)
    scores = jnp.einsum("rqd,rcd->rqc", group_query, keys[0], preferred_element_type=jnp.float32)
    scores = scores * (1.0 / head_depth**0.5)
    slot_ids = slot_first + jnp.arange(key_span, dtype=jnp.int32)
    live = (slot_ids[None, :] < lengths[:, None])[:, None, :]
    scores = jnp.where(live, scores, jnp.float32(-1e30))
    top_score = jnp.max(scores, axis=-1)
    weights = jnp.where(live, jnp.exp(scores - top_score[..., None]), jnp.float32(0.0))
    weight_total = jnp.sum(weights, axis=-1)
    weighted = jnp.einsum(
        "rqc,rcd->rqd", weights.astype(jnp.bfloat16), values[0], preferred_element_type=jnp.float32
    )
    state = (top_score, weight_total, weighted)
    for level in range(group_size.bit_length() - 1):
        partner = swapped(
            (for_sending(state[0]), for_sending(state[1]), for_sending(state[2])), "tensor", level
        )
        state = join_partial(state, partner)
    top_score, weight_total, weighted = state
    head_first = my_rank % group_size * heads_dev
    own_total = lax.dynamic_slice_in_dim(weight_total, head_first, heads_dev, 1)
    own_weighted = lax.dynamic_slice_in_dim(weighted, head_first, heads_dev, 1)
    attended = (
        (own_weighted / own_total[..., None])
        .reshape(row_count, heads_dev * head_depth)
        .astype(jnp.bfloat16)
    )
    projected = jnp.dot(attended, out_weight[0], preferred_element_type=jnp.float32)
    stream = residual[0].astype(jnp.float32)
    summed = lax.psum(projected.astype(jnp.bfloat16), "tensor").astype(jnp.float32)
    hidden = stream + summed
    scaled = (
        hidden * lax.rsqrt(jnp.mean(hidden * hidden, axis=-1, keepdims=True) + 1e-05) * norm_gain[0]
    )
    normed = scaled.astype(jnp.bfloat16)
    logits = jnp.dot(normed, head_weight[0], preferred_element_type=jnp.float32)
    vocab_local = logits.shape[1]
    vocab_ids = my_rank * vocab_local + jnp.arange(vocab_local, dtype=jnp.int32)
    target_hit = vocab_ids[None, :] == targets[:, None]
    pick_local = jnp.sum(jnp.where(target_hit, logits, jnp.float32(0.0)), axis=-1)
    top_logit = lax.pmax(jnp.max(logits, axis=-1), "tensor")
    exp_local = jnp.sum(jnp.exp(logits - top_logit[:, None]), axis=-1)
    exp_total, target_logit = lax.psum((exp_local, pick_local), "tensor")
    log_total = top_logit + jnp.log(exp_total)
    logprob = logits - log_total[:, None]
    target_own = target_logit - log_total
    half_rows = row_count // 2
    keep_first = member_rank * half_rows
    send_first = (1 - member_rank) * half_rows
    keep_logprob = lax.dynamic_slice_in_dim(logprob, keep_first, half_rows, 0)
    keep_target = lax.dynamic_slice_in_dim(target_own, keep_first, half_rows, 0)
    send_logprob = lax.dynamic_slice_in_dim(logprob, send_first, half_rows, 0)
    send_target = lax.dynamic_slice_in_dim(target_own, send_first, half_rows, 0)
    other_logprob, other_target = swapped((send_logprob, send_target), "member", 0)
    return (0.5 * (keep_logprob + other_logprob), 0.5 * (keep_target + other_target))


def solution(mesh):
    placed = (
        P("member", "rep", None, None),
        P("member", "rep", "tensor", None),
        P("member", "rep", "tensor", None),
        P("rep"),
        P("rep"),
        P("member", "rep", None),
        P("member", "tensor", None),
        P("member", None),
        P("member", None, "tensor"),
    )
    return jax.shard_map(
        local,
        mesh=mesh,
        in_specs=placed,
        out_specs=(P(("rep", "member"), "tensor"), P(("rep", "member"))),
        check_vma=False,
    )
```

profile of v0, /device:TPU:1, one launch (start us, length us, event | category | flops | bytes accessed | tf_op | source)
XLA Modules:
  0.0 211.9 jit_solution(13294165735235029691)
XLA Ops:
  7.3 0.9 broadcast_compare_fusion
  8.1 1.7 fusion.36
  9.8 0.2 fusion.7
  10.0 2.2 %collective-permute-start.4 = (bf16[8,8]{1,0:T(8,128)(2,1)S(1)}, bf16[8,8]{1,0:T(8,128)(2,1)S(1)}, u32[]{:S(2)}, u32[]{:S(2)}) collective-permute-start(bf16[8,8]{1,0:T(8,128)(2,1)S(1)} %convert_element_type.73), channel_id=1, source_target_pairs={{0,1},{1,0},{2,3},{3,2},{4,5},{5,4},{6,7},{7,6},{8,9},{9,8},{10,11... | collective-permute-start | bytes 392 | tf_op jit(solution)/shard_map/ppermute | solution.py:25
  12.4 1.5 fusion.37
  13.9 1.4 collective-permute-start.1
  15.3 2.7 %collective-permute-start.5 = (bf16[8,8]{1,0:T(8,128)(2,1)S(1)}, bf16[8,8]{1,0:T(8,128)(2,1)S(1)}, u32[]{:S(2)}, u32[]{:S(2)}) collective-permute-start(bf16[8,8]{1,0:T(8,128)(2,1)S(1)} %get-tuple-element.13), channel_id=1, source_target_pairs={{0,2},{2,0},{1,3},{3,1},{4,6},{6,4},{5,7},{7,5},{8,10},{10,8},{9,1... | collective-permute-start | bytes 392 | tf_op jit(solution)/shard_map/ppermute | solution.py:25
  18.0 0.3 collective-permute-start.2
  18.4 1.0 collective-permute-done.5
  19.4 2.6 %collective-permute-done.2 = bf16[8,8]{1,0:T(8,128)(2,1)S(1)} collective-permute-done((bf16[8,8]{1,0:T(8,128)(2,1)S(1)}, bf16[8,8]{1,0:T(8,128)(2,1)S(1)}, u32[]{:S(2)}, u32[]{:S(2)}) %collective-permute-start.2) | collective-permute-done | bytes 160 | tf_op jit(solution)/shard_map/ppermute | solution.py:25
  22.2 0.4 collective-permute-start.3
  22.7 3.7 %collective-permute-done.3 = bf16[8,8,128]{2,1,0:T(8,128)(2,1)S(1)} collective-permute-done((bf16[8,8,128]{2,1,0:T(8,128)(2,1)S(1)}, bf16[8,8,128]{2,1,0:T(8,128)(2,1)S(1)}, u32[]{:S(2)}, u32[]{:S(2)}) %collective-permute-start.3) | collective-permute-done | bytes 16416 | tf_op jit(solution)/shard_map/ppermute | solution.py:25
  26.5 1.0 convolution_convert_fusion
  27.5 93.4 %all-reduce.3.cloned.1.call-done = bf16[8,4096]{1,0:T(8,128)(2,1)} async-done(((bf16[8,4096]{1,0:T(8,128)(2,1)}), bf16[8,4096]{1,0:T(8,128)(2,1)}) %all-reduce.3.cloned.1.call-update) | async-done | bytes 65552 | tf_op jit(solution)/shard_map/psum | solution.py:80
  120.9 1.0 multiply_reduce_fusion
  121.9 4.8 %fusion.38 = (f32[8]{0:T(128)S(1)}, f32[8,1024]{1,0:T(8,128)S(1)}) fusion(bf16[1,4096,1024]{2,1,0:T(8,128)(2,1)} %param.17, bf16[8,4096]{1,0:T(8,128)(2,1)} %all-reduce.3.cloned.1.call-done, bf16[1,8,4096]{2,1,0:T(8,128)(2,1)} %param.14, f32[4096]{0:T(1024)} %bitcast.38, f32[8]{0:T(128)S(1)} %add_rsqrt_fusion), kind=kOutput, calls=%fused_computation.63 | convolution fusion | flops 67313656 | bytes 8568896 | tf_op jit(solution)/shard_map/dot_general | solution.py:86
  126.8 30.9 %pmax.7 = f32[8]{0:T(128)S(1)} all-reduce(f32[8]{0:T(128)S(1)} %get-tuple-element.21), channel_id=1, replica_groups=mesh['member'=2,'rep'=8,'tensor'=16] {'tensor'}, use_global_device_ids=true, to_apply=%region_5.6 | all-reduce | flops 8 | bytes 64 | tf_op jit(solution)/shard_map/pmax | solution.py:91
  157.6 0.2 select_reduce_fusion
  157.9 28.5 %all-reduce = (f32[8]{0:T(128)S(1)}, f32[8]{0:T(128)S(1)}) all-reduce(f32[8]{0:T(128)S(1)} %get-tuple-element.3, f32[8]{0:T(128)S(1)} %get-tuple-element.2), channel_id=1, replica_groups=mesh['member'=2,'rep'=8,'tensor'=16] {'tensor'}, use_global_device_ids=true, to_apply=%region_7.8 | all-reduce | flops 16 | bytes 128 | tf_op jit(solution)/shard_map/psum | solution.py:93
  186.5 16.5 %collective-permute-start.7 = (f32[4]{0:T(128)S(1)}, f32[4]{0:T(128)S(1)}, u32[]{:S(2)}, u32[]{:S(2)}) collective-permute-start(f32[4]{0:T(128)S(1)} %dynamic_slice.30), channel_id=1, source_target_pairs={{0,128},{128,0},{1,129},{129,1},{2,130},{130,2},{3,131},{131,3},{4... | collective-permute-start | bytes 56 | tf_op jit(solution)/shard_map/ppermute | solution.py:25
  203.0 0.1 collective-permute-start.6
  203.1 0.7 collective-permute-done.7
  203.8 0.6 add_multiply_fusion.1
  204.4 0.6 add_multiply_fusion
  (27 shorter events, 0.7 us)
Async XLA Ops:
  7.2 19.3 %copy-start = (bf16[1,256,4096]{2,1,0:T(8,128)(2,1)S(1)}, bf16[1,256,4096]{2,1,0:T(8,128)(2,1)}, u32[]{:S(2)}) copy-start(bf16[1,256,4096]{2,1,0:T(8,128)(2,1)} %param.15) | copy-start | bytes 6291460
  7.2 150.5 %copy-start.1 = (s32[8]{0:T(128)S(1)}, s32[8]{0:T(128)}, u32[]{:S(2)}) copy-start(s32[8]{0:T(128)} %param.13) | copy-start | bytes 100
  7.2 113.7 %all-reduce.3.cloned.1.call-start = ((), (), s32[]{:S(2)}) async-start(), calls=%async_computation | async-start | bytes 131072 | tf_op jit(solution)/shard_map/psum | solution.py:80
  10.0 5.3 %collective-permute-start.4 = (bf16[8,8]{1,0:T(8,128)(2,1)S(1)}, bf16[8,8]{1,0:T(8,128)(2,1)S(1)}, u32[]{:S(2)}, u32[]{:S(2)}) collective-permute-start(bf16[8,8]{1,0:T(8,128)(2,1)S(1)} %convert_element_type.73), channel_id=1, source_target_pairs={{0,1},{1,0},{2,3},{3,2},{4,5},{5,4},{6,7},{7,6},{8,9},{9,8},{10,11... | collective-permute-start | bytes 392 | tf_op jit(solution)/shard_map/ppermute | solution.py:25
  12.2 3.1 %collective-permute-start = (bf16[8,8]{1,0:T(8,128)(2,1)S(1)}, bf16[8,8]{1,0:T(8,128)(2,1)S(1)}, u32[]{:S(2)}, u32[]{:S(2)}) collective-permute-start(bf16[8,8]{1,0:T(8,128)(2,1)S(1)} %convert_element_type.65), channel_id=1, source_target_pairs={{0,1},{1,0},{2,3},{3,2},{4,5},{5,4},{6,7},{7,6},{8,9},{9,8},{10,11... | collective-permute-start | bytes 392 | tf_op jit(solution)/shard_map/ppermute | solution.py:25
  13.9 8.2 %collective-permute-start.1 = (bf16[8,8,128]{2,1,0:T(8,128)(2,1)S(1)}, bf16[8,8,128]{2,1,0:T(8,128)(2,1)S(1)}, u32[]{:S(2)}, u32[]{:S(2)}) collective-permute-start(bf16[8,8,128]{2,1,0:T(8,128)(2,1)S(1)} %get-tuple-element.19), channel_id=1, source_target_pairs={{0,1},{1,0},{2,3},{3,2},{4,5},{5,4},{6,7},{7,6},{8,9},{9,8},{10,11... | collective-permute-start | bytes 49160 | tf_op jit(solution)/shard_map/ppermute | solution.py:25
  15.3 4.0 %collective-permute-start.5 = (bf16[8,8]{1,0:T(8,128)(2,1)S(1)}, bf16[8,8]{1,0:T(8,128)(2,1)S(1)}, u32[]{:S(2)}, u32[]{:S(2)}) collective-permute-start(bf16[8,8]{1,0:T(8,128)(2,1)S(1)} %get-tuple-element.13), channel_id=1, source_target_pairs={{0,2},{2,0},{1,3},{3,1},{4,6},{6,4},{5,7},{7,5},{8,10},{10,8},{9,1... | collective-permute-start | bytes 392 | tf_op jit(solution)/shard_map/ppermute | solution.py:25
  18.0 3.9 %collective-permute-start.2 = (bf16[8,8]{1,0:T(8,128)(2,1)S(1)}, bf16[8,8]{1,0:T(8,128)(2,1)S(1)}, u32[]{:S(2)}, u32[]{:S(2)}) collective-permute-start(bf16[8,8]{1,0:T(8,128)(2,1)S(1)} %fusion.27), channel_id=1, source_target_pairs={{0,2},{2,0},{1,3},{3,1},{4,6},{6,4},{5,7},{7,5},{8,10},{10,8},{9,1... | collective-permute-start | bytes 392 | tf_op jit(solution)/shard_map/ppermute | solution.py:25
  22.2 4.2 %collective-permute-start.3 = (bf16[8,8,128]{2,1,0:T(8,128)(2,1)S(1)}, bf16[8,8,128]{2,1,0:T(8,128)(2,1)S(1)}, u32[]{:S(2)}, u32[]{:S(2)}) collective-permute-start(bf16[8,8,128]{2,1,0:T(8,128)(2,1)S(1)} %get-tuple-element.8), channel_id=1, source_target_pairs={{0,2},{2,0},{1,3},{3,1},{4,6},{6,4},{5,7},{7,5},{8,10},{10,8},{9,1... | collective-permute-start | bytes 49160 | tf_op jit(solution)/shard_map/ppermute | solution.py:25
  186.5 17.3 %collective-permute-start.7 = (f32[4]{0:T(128)S(1)}, f32[4]{0:T(128)S(1)}, u32[]{:S(2)}, u32[]{:S(2)}) collective-permute-start(f32[4]{0:T(128)S(1)} %dynamic_slice.30), channel_id=1, source_target_pairs={{0,128},{128,0},{1,129},{129,1},{2,130},{130,2},{3,131},{131,3},{4... | collective-permute-start | bytes 56 | tf_op jit(solution)/shard_map/ppermute | solution.py:25
  203.0 1.4 collective-permute-start.6
Sparse Core Ops, SparseCore 0:
  27.6 93.2 all-reduce.2
where the time goes:
time: 212 us
  waiting for transfers between devices  101 us (48%)
  blocking collectives  59.4 us (28%)
  starting transfers between devices  23.9 us (11%)
  between operations  14.1 us (7%)
  matrix products  9.04 us (4%)
  other arithmetic  3.79 us (2%)
    psum x1, waiting for transfers between devices, local(): lax.psum(projected.astype(jnp.bfloat16), 'tensor').astype(jnp.float32)  93.4 us
    pmax x1, blocking collectives, local(): top_logit = lax.pmax(jnp.max(logits, axis=-1), 'tensor')  30.9 us
    psum x1, blocking collectives, local(): exp_total, target_logit = lax.psum((exp_local, pick_local), 'tensor')  28.5 us
    ppermute x8, starting transfers between devices, swapped(): return lax.ppermute(block, axis, route)  23.8 us
    ppermute x8, waiting for transfers between devices, swapped(): return lax.ppermute(block, axis, route)  7.97 us
    dot_general x1, matrix products, local(): logits = jnp.dot(normed, head_weight[0], preferred_element_type=jnp.float32)  4.82 us
  transfers between devices with their start and end apart: 9, of which 5 were waited for; matrix products, arithmetic and copies ran while one was open for 1% of the time, Pallas kernels for 0%

commit v1 on v0

v1 whole, which is shorter than its diff:
```python
import functools

import jax
import jax.numpy as jnp
from jax import lax
from jax.experimental import pallas as pl
from jax.experimental.pallas import tpu as pltpu
from jax.sharding import PartitionSpec as P

HEADS = 32
KV_HEADS = 4
SIDE = 4
HBM = pltpu.MemorySpace.HBM

OFFSETS = sorted(
    [(dx, dy) for dx in range(SIDE) for dy in range(SIDE) if (dx, dy) != (0, 0)],
    key=lambda o: -(min(o[0], SIDE - o[0]) + min(o[1], SIDE - o[1])),
)


def slot_of(dx, dy):
    return (dx % SIDE) * SIDE + dy % SIDE


def step_kernel(
    q_hbm, k_hbm, v_hbm, len_hbm, tgt_hbm, res_hbm, wo_hbm, gain_hbm, wh_hbm,
    out_ref, tout_ref,
    q_ref, k_ref, v_ref, len_ref, tgt_ref, res_ref, wo_ref, gain_ref, inv_ref, wh_ref,
    att_send, att_recv, rs_send, rs_recv, hg_ref, lg_ref, lg_recv, stat_ref,
    in_sem, k_sem, v_sem, wh_sem,
    att_ssem, att_rsem, rs_ssem, rs_rsem, ag_ssem, ag_rsem, lg_ssem, lg_rsem, st_ssem, st_rsem,
):
    me = lax.axis_index("tensor")
    member = lax.axis_index("member")
    col, row = me // SIDE, me % SIDE
    rows, span, depth = k_ref.shape
    heads = HEADS // KV_HEADS
    width = wo_ref.shape[0]
    f32, bf16 = jnp.float32, jnp.bfloat16

    def peer(dx, dy):
        return (col + dx) % SIDE * SIDE + (row + dy) % SIDE

    small = [
        pltpu.make_async_copy(q_hbm.at[0, :, pl.ds(col * heads, heads), :], q_ref, in_sem.at[0]),
        pltpu.make_async_copy(len_hbm, len_ref, in_sem.at[1]),
        pltpu.make_async_copy(tgt_hbm, tgt_ref, in_sem.at[2]),
        pltpu.make_async_copy(
            res_hbm.at[0, :, pl.ds(pl.multiple_of(me * width, width), width)], res_ref, in_sem.at[3]
        ),
        pltpu.make_async_copy(gain_hbm, gain_ref, in_sem.at[4]),
        pltpu.make_async_copy(wo_hbm.at[0], wo_ref, in_sem.at[5]),
    ]
    k_copy = [
        pltpu.make_async_copy(k_hbm.at[0, r], k_ref.at[r], k_sem.at[r]) for r in range(rows)
    ]
    v_copy = [
        pltpu.make_async_copy(v_hbm.at[0, r], v_ref.at[r], v_sem.at[r]) for r in range(rows)
    ]
    chunks = wh_ref.shape[0] // width
    w_copy = [
        pltpu.make_async_copy(
            wh_hbm.at[0, pl.ds(c * width, width), :], wh_ref.at[pl.ds(c * width, width), :], wh_sem.at[c]
        )
        for c in range(chunks)
    ]
    small[0].start()
    small[1].start()
    for c in k_copy + v_copy:
        c.start()
    for c in small[2:]:
        c.start()

    barrier = pltpu.get_barrier_semaphore()
    for dx, dy in OFFSETS + [(0, 0)]:
        for other in range(2):
            if (dx, dy, other) == (0, 0, 0):
                continue
            pl.semaphore_signal(
                barrier,
                inc=1,
                device_id={"member": (member + other) % 2, "tensor": peer(dx, dy)},
                device_id_type=pl.DeviceIdType.MESH,
            )
    for c in w_copy:
        c.start()

    small[0].wait()
    small[1].wait()
    slot = row * span + lax.broadcasted_iota(jnp.int32, (heads, span), 1)
    lane = lax.broadcasted_iota(jnp.int32, (heads, depth), 1)
    scores, lives = [], []
    for r in range(rows):
        k_copy[r].wait()
        s = lax.dot_general(
            q_ref[r], k_ref[r], (((1,), (1,)), ((), ())), preferred_element_type=f32
        ) * (1.0 / depth**0.5)
        live = slot < len_ref[r]
        scores.append(jnp.where(live, s, f32(-1e30)))
        lives.append(live)
    for r in range(rows):
        top = jnp.max(scores[r], axis=-1, keepdims=True)
        w = jnp.where(lives[r], jnp.exp(scores[r] - top), f32(0.0))
        total = jnp.sum(w, axis=-1, keepdims=True)
        v_copy[r].wait()
        o = jnp.dot(w.astype(bf16), v_ref[r], preferred_element_type=f32)
        att_send[pl.ds(r, heads, stride=2 * rows), :] = o
        att_send[pl.ds(rows + r, heads, stride=2 * rows), :] = jnp.where(
            lane < depth // 2, top, total
        )

    pl.semaphore_wait(barrier, 31)
    block = 4 * rows
    att_copy = []
    for dy in (2, 1, 3):
        to = (row + dy) % SIDE
        att_copy.append(
            pltpu.make_async_remote_copy(
                src_ref=att_send.at[pl.ds(pl.multiple_of(to * block, block), block), :],
                dst_ref=att_recv.at[SIDE - dy - 1],
                send_sem=att_ssem.at[dy - 1],
                recv_sem=att_rsem.at[SIDE - dy - 1],
                device_id={"tensor": col * SIDE + to},
                device_id_type=pl.DeviceIdType.MESH,
            )
        )
        att_copy[-1].start()
    small[4].wait()
    inv_ref[...] = 1.0 / (gain_ref[...] * gain_ref[...])
    small[5].wait()
    small[2].wait()
    small[3].wait()
    parts = [att_send[pl.ds(pl.multiple_of(row * block, block), block), :]]
    for c in att_copy:
        c.wait_recv()
    for i in range(SIDE - 1):
        parts.append(att_recv[i])
    attended = []
    for h in range(2):
        base = 2 * h * rows
        stats = [p[base + rows : base + 2 * rows] for p in parts]
        peak = functools.reduce(jnp.maximum, stats)
        num, den = 0.0, 0.0
        for p, st in zip(parts, stats):
            scale = jnp.exp(st - peak)[:, 0:1]
            num = num + scale * p[base : base + rows]
            den = den + scale * st[:, depth // 2 : depth // 2 + 1]
        attended.append(num / den)
    attended = jnp.concatenate(attended, axis=1).astype(bf16)

    def project(t):
        return jnp.dot(
            attended,
            wo_ref[:, pl.ds(pl.multiple_of(t * width, width), width)],
            preferred_element_type=f32,
        )

    rs_copy = []
    for dx, dy in OFFSETS:
        t = peer(dx, dy)
        here, there = slot_of(dx, dy) - 1, slot_of(-dx, -dy) - 1
        rs_send[here] = project(t).astype(bf16)
        rs_copy.append(
            pltpu.make_async_remote_copy(
                src_ref=rs_send.at[here],
                dst_ref=rs_recv.at[there],
                send_sem=rs_ssem.at[here],
                recv_sem=rs_rsem.at[there],
                device_id={"tensor": t},
                device_id_type=pl.DeviceIdType.MESH,
            )
        )
        rs_copy[-1].start()
    hidden = project(me) + res_ref[...].astype(f32)
    for c in rs_copy[::-1]:
        c.wait_recv()
    for i in range(rs_recv.shape[0]):
        hidden = hidden + rs_recv[i].astype(f32)
    gain = gain_ref[:, pl.ds(pl.multiple_of(me * width, width), width)]
    hg_ref[0] = (hidden * gain).astype(bf16)
    ag_copy = {}
    for dx, dy in OFFSETS:
        here, there = slot_of(dx, dy), slot_of(-dx, -dy)
        ag_copy[there] = pltpu.make_async_remote_copy(
            src_ref=hg_ref.at[0],
            dst_ref=hg_ref.at[there],
            send_sem=ag_ssem.at[there - 1],
            recv_sem=ag_rsem.at[there - 1],
            device_id={"tensor": peer(dx, dy)},
            device_id_type=pl.DeviceIdType.MESH,
        )
        ag_copy[there].start()

    for c in w_copy:
        c.wait()
    logits, square = 0.0, 0.0
    for dx, dy in [(0, 0)] + OFFSETS[::-1]:
        t, k = peer(dx, dy), slot_of(dx, dy)
        if k:
            ag_copy[k].wait_recv()
        here = pl.multiple_of(t * width, width)
        part = hg_ref[k]
        logits = logits + jnp.dot(part, wh_ref[pl.ds(here, width), :], preferred_element_type=f32)
        wide = part.astype(f32)
        square = square + wide * wide * inv_ref[:, pl.ds(here, width)]
    mean_square = jnp.sum(square, axis=-1, keepdims=True) * (1.0 / (chunks * width))
    logits = logits * lax.rsqrt(mean_square + 1e-05)
    half = rows // 2
    lg_ref[0] = logits[:half]
    lg_ref[1] = logits[half:]
    lg_copy = pltpu.make_async_remote_copy(
        src_ref=lg_ref.at[1 - member],
        dst_ref=lg_recv,
        send_sem=lg_ssem,
        recv_sem=lg_rsem,
        device_id={"member": 1 - member},
        device_id_type=pl.DeviceIdType.MESH,
    )
    lg_copy.start()

    vocab = logits.shape[1]
    ids = me * vocab + lax.broadcasted_iota(jnp.int32, (rows, vocab), 1)
    sub = lax.broadcasted_iota(jnp.int32, (rows, 1), 0)
    want = jnp.zeros((rows, 1), jnp.int32)
    for r in range(rows):
        want = jnp.where(sub == r, tgt_ref[r], want)
    pick = jnp.sum(jnp.where(ids == want, logits, f32(0.0)), axis=-1, keepdims=True)
    top = jnp.max(logits, axis=-1, keepdims=True)
    lse = top + jnp.log(jnp.sum(jnp.exp(logits - top), axis=-1, keepdims=True))
    lanes = lax.broadcasted_iota(jnp.int32, (rows, 128), 1)
    subs = lax.broadcasted_iota(jnp.int32, (rows, 128), 0)
    spread = jnp.where(lanes < 64, lse, pick)
    stat_ref[0] = jnp.sum(
        jnp.where(lanes // 8 % 8 == subs, spread, f32(0.0)), axis=0, keepdims=True
    )
    st_copy = []
    for dx, dy in OFFSETS + [(0, 0)]:
        for other in range(2):
            there = slot_of(-dx, -dy) + SIDE * SIDE * other
            if there == 0:
                continue
            st_copy.append(
                pltpu.make_async_remote_copy(
                    src_ref=stat_ref.at[0],
                    dst_ref=stat_ref.at[there],
                    send_sem=st_ssem.at[there - 1],
                    recv_sem=st_rsem.at[there - 1],
                    device_id={"member": (member + other) % 2, "tensor": peer(dx, dy)},
                    device_id_type=pl.DeviceIdType.MESH,
                )
            )
            st_copy[-1].start()
    lg_copy.wait_recv()
    mean_logits = 0.5 * (lg_ref[member] + lg_recv[...])
    for c in st_copy[::-1]:
        c.wait_recv()
    log_total, target = 0.0, 0.0
    for other in range(2):
        got = [stat_ref[other * SIDE * SIDE + i] for i in range(SIDE * SIDE)]
        peak = functools.reduce(jnp.maximum, got)
        log_total = log_total + 0.5 * (peak + jnp.log(sum(jnp.exp(g - peak) for g in got)))
        target = target + 0.5 * sum(got)
    lanes = lax.broadcasted_iota(jnp.int32, (half, 128), 1)
    mine = 8 * (member * half + lax.broadcasted_iota(jnp.int32, (half, 128), 0))
    shift = jnp.sum(jnp.where(lanes == mine, log_total, f32(0.0)), axis=-1, keepdims=True)
    chosen = jnp.sum(jnp.where(lanes == mine + 64, target, f32(0.0)), axis=-1, keepdims=True)
    out_ref[...] = mean_logits - shift
    tout_ref[...] = jnp.broadcast_to(chosen - shift, (half, 128))

    for c in att_copy + rs_copy + list(ag_copy.values()) + [lg_copy] + st_copy:
        c.wait_send()


def local(queries, keys, values, lengths, targets, residual, out_weight, norm_gain, head_weight):
    rows, span, depth = keys.shape[1:]
    width, model = out_weight.shape[1:]
    vocab = head_weight.shape[2]
    peers = SIDE * SIDE - 1
    heads = HEADS // KV_HEADS
    f32, bf16 = jnp.float32, jnp.bfloat16
    dma = pltpu.SemaphoreType.DMA
    out, target = pl.pallas_call(
        step_kernel,
        out_shape=(
            jax.ShapeDtypeStruct((rows // 2, vocab), f32),
            jax.ShapeDtypeStruct((rows // 2, 128), f32),
        ),
        in_specs=[pl.BlockSpec(memory_space=HBM)] * 9,
        out_specs=(
            pl.BlockSpec(memory_space=pltpu.MemorySpace.VMEM),
            pl.BlockSpec(memory_space=pltpu.MemorySpace.VMEM),
        ),
        scratch_shapes=[
            pltpu.VMEM((rows, heads, depth), bf16),
            pltpu.VMEM((rows, span, depth), bf16),
            pltpu.VMEM((rows, span, depth), bf16),
            pltpu.SMEM((rows,), jnp.int32),
            pltpu.SMEM((rows,), jnp.int32),
            pltpu.VMEM((rows, width), bf16),
            pltpu.VMEM((width, model), bf16),
            pltpu.VMEM((1, model), f32),
            pltpu.VMEM((1, model), f32),
            pltpu.VMEM((model, vocab), bf16),
            pltpu.VMEM((2 * heads * rows, depth), f32),
            pltpu.VMEM((SIDE - 1, 4 * rows, depth), f32),
            pltpu.VMEM((peers, rows, width), bf16),
            pltpu.VMEM((peers, rows, width), bf16),
            pltpu.VMEM((peers + 1, rows, width), bf16),
            pltpu.VMEM((2, rows // 2, vocab), f32),
            pltpu.VMEM((rows // 2, vocab), f32),
            pltpu.VMEM((2 * (peers + 1), 1, 128), f32),
            dma((6,)), dma((rows,)), dma((rows,)), dma((peers + 1,)),
            dma((SIDE - 1,)), dma((SIDE - 1,)),
            dma((peers,)), dma((peers,)),
            dma((peers,)), dma((peers,)),
            dma, dma,
            dma((2 * peers + 1,)), dma((2 * peers + 1,)),
        ],
        compiler_params=pltpu.CompilerParams(
            collective_id=0, has_side_effects=True, vmem_limit_bytes=62 << 20
        ),
        name="decode_step",
    )(queries, keys, values, lengths, targets, residual, out_weight, norm_gain, head_weight)
    return out, target[:, 0]


def solution(mesh):
    placed = (
        P("member", "rep", None, None),
        P("member", "rep", "tensor", None),
        P("member", "rep", "tensor", None),
        P("rep"),
        P("rep"),
        P("member", "rep", None),
        P("member", "tensor", None),
        P("member", None),
        P("member", None, "tensor"),
    )
    return jax.shard_map(
        local,
        mesh=mesh,
        in_specs=placed,
        out_specs=(P(("rep", "member"), "tensor"), P(("rep", "member"))),
        check_vma=False,
    )
```

time: 212 us -> 31.3 us (0.15)
  waiting for transfers between devices: 101 us -> 0 us
  blocking collectives: 59.4 us -> 0 us
  Pallas kernels: 0 us -> 27.8 us
  starting transfers between devices: 23.9 us -> 0 us
  between operations: 14.1 us -> 0.64 us
  matrix products: 9.04 us -> 0 us
  other arithmetic: 3.79 us -> 0 us
  local copies, waits for them, and re-layouts: 0.24 us -> 2.62 us
    psum x1 -> x0, waiting for transfers between devices: 93.4 us -> none  [local(): lax.psum(projected.astype(jnp.bfloat16), 'tensor').astype(jnp.float32)]
    pmax x1 -> x0, blocking collectives: 30.9 us -> none  [local(): top_logit = lax.pmax(jnp.max(logits, axis=-1), 'tensor')]
    psum x1 -> x0, blocking collectives: 28.5 us -> none  [local(): exp_total, target_logit = lax.psum((exp_local, pick_local), 'tensor')]
    pallas_call x0 -> x1, Pallas kernels: none -> 27.8 us  [local(): pl.pallas_call(step_kernel, out_shape=(jax.ShapeDtypeStruct((rows // 2, v...]
    ppermute x8 -> x0, starting transfers between devices: 23.8 us -> none  [swapped(): return lax.ppermute(block, axis, route)]
    dot_general x4 -> x0, matrix products: 9.04 us -> none  [the longest x1 4.82 us: local(): logits = jnp.dot(normed, head_weight[0], preferred_element_type=jnp.float32)]
    ppermute x8 -> x0, waiting for transfers between devices: 7.97 us -> none  [swapped(): return lax.ppermute(block, axis, route)]
  transfers between devices with their start and end apart: 9 -> 0, of which waited for: 5 -> 0; matrix products, arithmetic and copies ran while one was open for 1% -> 0% of each run, Pallas kernels for 0% -> 0%
where the time goes in v1:
time: 31.3 us; the launch traced here: 31.1 us
  Pallas kernels  27.8 us (89%)
  local copies, waits for them, and re-layouts  2.62 us (8%)
  between operations  0.64 us (2%)
    pallas_call x1, Pallas kernels, local(): pl.pallas_call(step_kernel, out_shape=(jax.ShapeDtypeStruct((rows // 2, v...  27.8 us
    unnamed x1, local copies, waits for them, and re-layouts  1.32 us
    slice x1, local copies, waits for them, and re-layouts, local(): return (out, target[:, 0])  1.3 us

profile of v1, /device:TPU:1, one launch (start us, length us, event | category | flops | bytes accessed | tf_op | source)
XLA Modules:
  0.0 31.1 jit_solution(5327410767252237898)
XLA Ops:
  0.6 27.8 %decode_step.1 = (f32[4,1024]{1,0:T(4,128)}, f32[4,128]{1,0:T(4,128)}) custom-call(bf16[1,8,32,128]{3,2,1,0:T(8,128)(2,1)} %q_hbm.1, bf16[1,8,512,128]{3,2,1,0:T(8,128)(2,1)} %k_hbm.1, bf16[1,8,512,128]{3,2,1,0:T(8,128)(2,1)} %v_hbm.1, s32[8]{0:T(128)} %len_hbm.1, s32[8]{0:T(128)} %tgt_hbm.1, bf16[1,8,4096]{2,1,0:T(8,128)(2,1)} %res_hbm.1, ...), custom_call_target="tpu_custom_call" | custom-call | tf_op jit(solution)/shard_map/decode_step/pallas_call | solution.py:282
  28.5 1.3 %slice_reduce_fusion = f32[4]{0:T(128)} fusion(f32[4,128]{1,0:T(4,128)} %get-tuple-element.5), kind=kLoop, calls=%fused_computation | loop fusion | bytes 32 | tf_op jit(solution)/shard_map/slice | solution.py:324
  29.8 1.3 %copy.12 = f32[4,1024]{1,0:T(4,128)} copy(f32[4,1024]{1,0:T(4,128)} %get-tuple-element.8) | data formatting | bytes 32768

commit v2 on v1

--- a/solution.py
+++ b/solution.py
@@ -10,11 +10,17 @@
 HEADS = 32
 KV_HEADS = 4
 SIDE = 4
+CHUNKS = 4
 HBM = pltpu.MemorySpace.HBM
+
+
+def hops(dx, dy):
+    return min(dx, SIDE - dx) + min(dy, SIDE - dy)
+
 
 OFFSETS = sorted(
     [(dx, dy) for dx in range(SIDE) for dy in range(SIDE) if (dx, dy) != (0, 0)],
-    key=lambda o: -(min(o[0], SIDE - o[0]) + min(o[1], SIDE - o[1])),
+    key=lambda o: -hops(*o),
 )
 
 
@@ -26,9 +32,9 @@
     q_hbm, k_hbm, v_hbm, len_hbm, tgt_hbm, res_hbm, wo_hbm, gain_hbm, wh_hbm,
     out_ref, tout_ref,
     q_ref, k_ref, v_ref, len_ref, tgt_ref, res_ref, wo_ref, gain_ref, inv_ref, wh_ref,
-    att_send, att_recv, rs_send, rs_recv, hg_ref, lg_ref, lg_recv, stat_ref,
+    res_other, gain_other, att_send, att_recv, rs_send, rs_recv, ag_ref, hg_ref, lg_ref, lg_recv, stat_ref,
     in_sem, k_sem, v_sem, wh_sem,
-    att_ssem, att_rsem, rs_ssem, rs_rsem, ag_ssem, ag_rsem, lg_ssem, lg_rsem, st_ssem, st_rsem,
+    side_ssem, side_rsem, att_ssem, att_rsem, rs_ssem, rs_rsem, ag_ssem, ag_rsem, lg_ssem, lg_rsem, st_ssem, st_rsem,
 ):
     me = lax.axis_index("tensor")
     member = lax.axis_index("member")
@@ -51,18 +57,23 @@
         pltpu.make_async_copy(gain_hbm, gain_ref, in_sem.at[4]),
         pltpu.make_async_copy(wo_hbm.at[0], wo_ref, in_sem.at[5]),
     ]
-    k_copy = [
-        pltpu.make_async_copy(k_hbm.at[0, r], k_ref.at[r], k_sem.at[r]) for r in range(rows)
+    half = rows // 2
+    k_copy, v_copy = [
+        [
+            pltpu.make_async_copy(
+                hbm.at[0, pl.ds(i * half, half)], ref.at[pl.ds(i * half, half)], sem.at[i]
+            )
+            for i in range(2)
+        ]
+        for hbm, ref, sem in ((k_hbm, k_ref, k_sem), (v_hbm, v_ref, v_sem))
     ]
-    v_copy = [
-        pltpu.make_async_copy(v_hbm.at[0, r], v_ref.at[r], v_sem.at[r]) for r in range(rows)
-    ]
-    chunks = wh_ref.shape[0] // width
+    model = wh_ref.shape[0]
+    chunk = model // CHUNKS
     w_copy = [
         pltpu.make_async_copy(
-            wh_hbm.at[0, pl.ds(c * width, width), :], wh_ref.at[pl.ds(c * width, width), :], wh_sem.at[c]
-        )
-        for c in range(chunks)
+            wh_hbm.at[0, pl.ds(c * chunk, chunk), :], wh_ref.at[pl.ds(c * chunk, chunk), :], wh_sem.at[c]
+        )
+        for c in range(CHUNKS)
     ]
     small[0].start()
     small[1].start()
@@ -89,24 +100,27 @@
     small[1].wait()
     slot = row * span + lax.broadcasted_iota(jnp.int32, (heads, span), 1)
     lane = lax.broadcasted_iota(jnp.int32, (heads, depth), 1)
-    scores, lives = [], []
+    weights = []
     for r in range(rows):
-        k_copy[r].wait()
+        if r % half == 0:
+            k_copy[r // half].wait()
         s = lax.dot_general(
             q_ref[r], k_ref[r], (((1,), (1,)), ((), ())), preferred_element_type=f32
         ) * (1.0 / depth**0.5)
         live = slot < len_ref[r]
-        scores.append(jnp.where(live, s, f32(-1e30)))
-        lives.append(live)
-    for r in range(rows):
-        top = jnp.max(scores[r], axis=-1, keepdims=True)
-        w = jnp.where(lives[r], jnp.exp(scores[r] - top), f32(0.0))
+        s = jnp.where(live, s, f32(-1e30))
+        top = jnp.max(s, axis=-1, keepdims=True)
+        w = jnp.where(live, jnp.exp(s - top), f32(0.0))
         total = jnp.sum(w, axis=-1, keepdims=True)
-        v_copy[r].wait()
-        o = jnp.dot(w.astype(bf16), v_ref[r], preferred_element_type=f32)
-        att_send[pl.ds(r, heads, stride=2 * rows), :] = o
+        weights.append(w.astype(bf16))
         att_send[pl.ds(rows + r, heads, stride=2 * rows), :] = jnp.where(
             lane < depth // 2, top, total
+        )
+    for c in v_copy:
+        c.wait()
+    for r in range(rows):
+        att_send[pl.ds(r, heads, stride=2 * rows), :] = jnp.dot(
+            weights[r], v_ref[r], preferred_element_type=f32
         )
 
     pl.semaphore_wait(barrier, 31)
@@ -125,11 +139,25 @@
             )
         )
         att_copy[-1].start()
+    small[3].wait()
     small[4].wait()
+    mine = pl.ds(pl.multiple_of(me * width, width), width)
+    side_copy = [
+        pltpu.make_async_remote_copy(
+            src_ref=src,
+            dst_ref=dst,
+            send_sem=side_ssem.at[i],
+            recv_sem=side_rsem.at[i],
+            device_id={"member": 1 - member},
+            device_id_type=pl.DeviceIdType.MESH,
+        )
+        for i, (src, dst) in enumerate([(res_ref, res_other), (gain_ref.at[:, mine], gain_other)])
+    ]
+    for c in side_copy:
+        c.start()
     inv_ref[...] = 1.0 / (gain_ref[...] * gain_ref[...])
     small[5].wait()
     small[2].wait()
-    small[3].wait()
     parts = [att_send[pl.ds(pl.multiple_of(row * block, block), block), :]]
     for c in att_copy:
         c.wait_recv()
@@ -156,9 +184,9 @@
         )
 
     rs_copy = []
-    for dx, dy in OFFSETS:
+    for dx, dy in OFFSETS + [(0, 0)]:
         t = peer(dx, dy)
-        here, there = slot_of(dx, dy) - 1, slot_of(-dx, -dy) - 1
+        here, there = slot_of(dx, dy), slot_of(-dx, -dy)
         rs_send[here] = project(t).astype(bf16)
         rs_copy.append(
             pltpu.make_async_remote_copy(
@@ -166,27 +194,28 @@
                 dst_ref=rs_recv.at[there],
                 send_sem=rs_ssem.at[here],
                 recv_sem=rs_rsem.at[there],
-                device_id={"tensor": t},
+                device_id={"member": 1 - member, "tensor": t},
                 device_id_type=pl.DeviceIdType.MESH,
             )
         )
         rs_copy[-1].start()
-    hidden = project(me) + res_ref[...].astype(f32)
+    for c in side_copy:
+        c.wait_recv()
+    hidden = res_other[...].astype(f32)
     for c in rs_copy[::-1]:
         c.wait_recv()
     for i in range(rs_recv.shape[0]):
         hidden = hidden + rs_recv[i].astype(f32)
-    gain = gain_ref[:, pl.ds(pl.multiple_of(me * width, width), width)]
-    hg_ref[0] = (hidden * gain).astype(bf16)
+    ag_ref[...] = (hidden * gain_other[...]).astype(bf16)
     ag_copy = {}
-    for dx, dy in OFFSETS:
-        here, there = slot_of(dx, dy), slot_of(-dx, -dy)
+    for dx, dy in OFFSETS + [(0, 0)]:
+        there = slot_of(-dx, -dy)
         ag_copy[there] = pltpu.make_async_remote_copy(
-            src_ref=hg_ref.at[0],
+            src_ref=ag_ref,
             dst_ref=hg_ref.at[there],
-            send_sem=ag_ssem.at[there - 1],
-            recv_sem=ag_rsem.at[there - 1],
-            device_id={"tensor": peer(dx, dy)},
+            send_sem=ag_ssem.at[there],
+            recv_sem=ag_rsem.at[there],
+            device_id={"member": 1 - member, "tensor": peer(dx, dy)},
             device_id_type=pl.DeviceIdType.MESH,
         )
         ag_copy[there].start()
@@ -194,18 +223,20 @@
     for c in w_copy:
         c.wait()
     logits, square = 0.0, 0.0
-    for dx, dy in [(0, 0)] + OFFSETS[::-1]:
+    nearest = [(0, 0)] + OFFSETS[::-1]
+    for i, (dx, dy) in enumerate(nearest):
+        if i == 0 or hops(dx, dy) != hops(*nearest[i - 1]):
+            for o in nearest:
+                if hops(*o) == hops(dx, dy):
+                    ag_copy[slot_of(*o)].wait_recv()
         t, k = peer(dx, dy), slot_of(dx, dy)
-        if k:
-            ag_copy[k].wait_recv()
         here = pl.multiple_of(t * width, width)
         part = hg_ref[k]
         logits = logits + jnp.dot(part, wh_ref[pl.ds(here, width), :], preferred_element_type=f32)
         wide = part.astype(f32)
         square = square + wide * wide * inv_ref[:, pl.ds(here, width)]
-    mean_square = jnp.sum(square, axis=-1, keepdims=True) * (1.0 / (chunks * width))
+    mean_square = jnp.sum(square, axis=-1, keepdims=True) * (1.0 / model)
     logits = logits * lax.rsqrt(mean_square + 1e-05)
-    half = rows // 2
     lg_ref[0] = logits[:half]
     lg_ref[1] = logits[half:]
     lg_copy = pltpu.make_async_remote_copy(
@@ -267,7 +298,7 @@
     out_ref[...] = mean_logits - shift
     tout_ref[...] = jnp.broadcast_to(chosen - shift, (half, 128))
 
-    for c in att_copy + rs_copy + list(ag_copy.values()) + [lg_copy] + st_copy:
+    for c in att_copy + side_copy + rs_copy + list(ag_copy.values()) + [lg_copy] + st_copy:
         c.wait_send()
 
 
@@ -301,26 +332,29 @@
             pltpu.VMEM((1, model), f32),
             pltpu.VMEM((1, model), f32),
             pltpu.VMEM((model, vocab), bf16),
+            pltpu.VMEM((rows, width), bf16),
+            pltpu.VMEM((1, width), f32),
             pltpu.VMEM((2 * heads * rows, depth), f32),
             pltpu.VMEM((SIDE - 1, 4 * rows, depth), f32),
-            pltpu.VMEM((peers, rows, width), bf16),
-            pltpu.VMEM((peers, rows, width), bf16),
+            pltpu.VMEM((peers + 1, rows, width), bf16),
+            pltpu.VMEM((peers + 1, rows, width), bf16),
+            pltpu.VMEM((rows, width), bf16),
             pltpu.VMEM((peers + 1, rows, width), bf16),
             pltpu.VMEM((2, rows // 2, vocab), f32),
             pltpu.VMEM((rows // 2, vocab), f32),
             pltpu.VMEM((2 * (peers + 1), 1, 128), f32),
-            dma((6,)), dma((rows,)), dma((rows,)), dma((peers + 1,)),
-            dma((SIDE - 1,)), dma((SIDE - 1,)),
-            dma((peers,)), dma((peers,)),
-            dma((peers,)), dma((peers,)),
+            dma((6,)), dma((2,)), dma((2,)), dma((CHUNKS,)),
+            dma((2,)), dma((2,)), dma((SIDE - 1,)), dma((SIDE - 1,)),
+            dma((peers + 1,)), dma((peers + 1,)),
+            dma((peers + 1,)), dma((peers + 1,)),
             dma, dma,
             dma((2 * peers + 1,)), dma((2 * peers + 1,)),
         ],
         compiler_params=pltpu.CompilerParams(
-            collective_id=0, has_side_effects=True, vmem_limit_bytes=62 << 20
+            collective_id=0, has_side_effects=True, vmem_limit_bytes=48 << 20
         ),
         name="decode_step",
-    )(queries, keys, values, lengths, targets, residual, out_weight, norm_gain, head_weight)
+    )(*(pltpu.with_memory_space_constraint(a, HBM) for a in (queries, keys, values, lengths, targets, residual, out_weight, norm_gain, head_weight)))
     return out, target[:, 0]
 
 

time: 31.3 us -> 28.4 us (0.907)
  local copies, waits for them, and re-layouts: 2.62 us -> 1.23 us
  Pallas kernels: 27.8 us -> 26.5 us
    pallas_call x1, Pallas kernels: 27.8 us -> 26.5 us  [local(): pl.pallas_call(step_kernel, out_shape=(jax.ShapeDtypeStruct((rows // 2, v...]
    unnamed x1, local copies, waits for them, and re-layouts: 1.32 us -> 0.6 us
    slice x1, local copies, waits for them, and re-layouts: 1.3 us -> 0.63 us  [local(): return (out, target[:, 0])]
where the time goes in v2:
time: 28.4 us; the launch traced here: 28.3 us
  Pallas kernels  26.5 us (93%)
  local copies, waits for them, and re-layouts  1.23 us (4%)
  between operations  0.64 us (2%)
    pallas_call x1, Pallas kernels, local(): pl.pallas_call(step_kernel, out_shape=(jax.ShapeDtypeStruct((rows // 2, v...  26.5 us
    slice x1, local copies, waits for them, and re-layouts, local(): return (out, target[:, 0])  0.63 us
    unnamed x1, local copies, waits for them, and re-layouts  0.6 us

profile of v2, /device:TPU:1, one launch (start us, length us, event | category | flops | bytes accessed | tf_op | source)
XLA Modules:
  0.0 28.3 jit_solution(14531348539186101883)
XLA Ops:
  0.6 26.5 %decode_step.1 = (f32[4,1024]{1,0:T(4,128)S(1)}, f32[4,128]{1,0:T(4,128)S(1)}) custom-call(bf16[1,8,32,128]{3,2,1,0:T(8,128)(2,1)} %q_hbm.1, bf16[1,8,512,128]{3,2,1,0:T(8,128)(2,1)} %k_hbm.1, bf16[1,8,512,128]{3,2,1,0:T(8,128)(2,1)} %v_hbm.1, s32[8]{0:T(128)} %len_hbm.1, s32[8]{0:T(128)} %tgt_hbm.1, bf16[1,8,4096]{2,1,0:T(8,128)(2,1)} %res_hbm.1, ...), custom_call_target="tpu_custom_call" | custom-call | tf_op jit(solution)/shard_map/decode_step/pallas_call | solution.py:313
  27.1 0.6 %slice_reduce_fusion = f32[4]{0:T(128)} fusion(f32[4,128]{1,0:T(4,128)S(1)} %get-tuple-element.5), kind=kLoop, calls=%fused_computation | loop fusion | bytes 32 | tf_op jit(solution)/shard_map/slice | solution.py:358
  27.7 0.6 %copy.12 = f32[4,1024]{1,0:T(4,128)} copy(f32[4,1024]{1,0:T(4,128)S(1)} %get-tuple-element.8) | data formatting | bytes 32768

commit v3 on v2

--- a/solution.py
+++ b/solution.py
@@ -24,8 +24,17 @@
 )
 
 
+NEAREST = [(0, 0)] + OFFSETS[::-1]
+SLOT = {o: i for i, o in enumerate(NEAREST)}
+REACH = [[i for i, o in enumerate(NEAREST) if hops(*o) == n] for n in range(SIDE + 1)]
+
+
 def slot_of(dx, dy):
-    return (dx % SIDE) * SIDE + dy % SIDE
+    return SLOT[dx % SIDE, dy % SIDE]
+
+
+def arrival(ref, sem):
+    return pltpu.make_async_copy(ref, ref, sem)
 
 
 def step_kernel(
@@ -58,32 +67,23 @@
         pltpu.make_async_copy(wo_hbm.at[0], wo_ref, in_sem.at[5]),
     ]
     half = rows // 2
-    k_copy, v_copy = [
-        [
-            pltpu.make_async_copy(
-                hbm.at[0, pl.ds(i * half, half)], ref.at[pl.ds(i * half, half)], sem.at[i]
-            )
-            for i in range(2)
-        ]
-        for hbm, ref, sem in ((k_hbm, k_ref, k_sem), (v_hbm, v_ref, v_sem))
-    ]
+    k_copy = pltpu.make_async_copy(k_hbm.at[0], k_ref, k_sem)
+    v_copy = pltpu.make_async_copy(v_hbm.at[0], v_ref, v_sem)
     model = wh_ref.shape[0]
     chunk = model // CHUNKS
     w_copy = [
         pltpu.make_async_copy(
-            wh_hbm.at[0, pl.ds(c * chunk, chunk), :], wh_ref.at[pl.ds(c * chunk, chunk), :], wh_sem.at[c]
+            wh_hbm.at[0, pl.ds(c * chunk, chunk), :], wh_ref.at[pl.ds(c * chunk, chunk), :], wh_sem
         )
         for c in range(CHUNKS)
     ]
     small[0].start()
     small[1].start()
-    for c in k_copy + v_copy:
-        c.start()
-    for c in small[2:]:
-        c.start()
-
+    k_copy.start()
+    v_copy.start()
     barrier = pltpu.get_barrier_semaphore()
-    for dx, dy in OFFSETS + [(0, 0)]:
+    near = [o for o in OFFSETS + [(0, 0)] if 0 in o]
+    for dx, dy in near:
         for other in range(2):
             if (dx, dy, other) == (0, 0, 0):
                 continue
@@ -93,17 +93,16 @@
                 device_id={"member": (member + other) % 2, "tensor": peer(dx, dy)},
                 device_id_type=pl.DeviceIdType.MESH,
             )
-    for c in w_copy:
+    for c in small[2:] + w_copy:
         c.start()
 
     small[0].wait()
     small[1].wait()
+    k_copy.wait()
     slot = row * span + lax.broadcasted_iota(jnp.int32, (heads, span), 1)
     lane = lax.broadcasted_iota(jnp.int32, (heads, depth), 1)
     weights = []
     for r in range(rows):
-        if r % half == 0:
-            k_copy[r // half].wait()
         s = lax.dot_general(
             q_ref[r], k_ref[r], (((1,), (1,)), ((), ())), preferred_element_type=f32
         ) * (1.0 / depth**0.5)
@@ -116,29 +115,24 @@
         att_send[pl.ds(rows + r, heads, stride=2 * rows), :] = jnp.where(
             lane < depth // 2, top, total
         )
-    for c in v_copy:
-        c.wait()
+    v_copy.wait()
     for r in range(rows):
         att_send[pl.ds(r, heads, stride=2 * rows), :] = jnp.dot(
             weights[r], v_ref[r], preferred_element_type=f32
         )
 
-    pl.semaphore_wait(barrier, 31)
+    pl.semaphore_wait(barrier, 2 * len(near) - 1)
     block = 4 * rows
-    att_copy = []
     for dy in (2, 1, 3):
         to = (row + dy) % SIDE
-        att_copy.append(
-            pltpu.make_async_remote_copy(
-                src_ref=att_send.at[pl.ds(pl.multiple_of(to * block, block), block), :],
-                dst_ref=att_recv.at[SIDE - dy - 1],
-                send_sem=att_ssem.at[dy - 1],
-                recv_sem=att_rsem.at[SIDE - dy - 1],
-                device_id={"tensor": col * SIDE + to},
-                device_id_type=pl.DeviceIdType.MESH,
-            )
-        )
-        att_copy[-1].start()
+        pltpu.make_async_remote_copy(
+            src_ref=att_send.at[pl.ds(pl.multiple_of(to * block, block), block), :],
+            dst_ref=att_recv.at[SIDE - dy - 1],
+            send_sem=att_ssem,
+            recv_sem=att_rsem,
+            device_id={"tensor": col * SIDE + to},
+            device_id_type=pl.DeviceIdType.MESH,
+        ).start()
     small[3].wait()
     small[4].wait()
     mine = pl.ds(pl.multiple_of(me * width, width), width)
@@ -159,8 +153,7 @@
     small[5].wait()
     small[2].wait()
     parts = [att_send[pl.ds(pl.multiple_of(row * block, block), block), :]]
-    for c in att_copy:
-        c.wait_recv()
+    arrival(att_recv, att_rsem).wait()
     for i in range(SIDE - 1):
         parts.append(att_recv[i])
     attended = []
@@ -183,53 +176,43 @@
             preferred_element_type=f32,
         )
 
-    rs_copy = []
     for dx, dy in OFFSETS + [(0, 0)]:
         t = peer(dx, dy)
         here, there = slot_of(dx, dy), slot_of(-dx, -dy)
         rs_send[here] = project(t).astype(bf16)
-        rs_copy.append(
-            pltpu.make_async_remote_copy(
-                src_ref=rs_send.at[here],
-                dst_ref=rs_recv.at[there],
-                send_sem=rs_ssem.at[here],
-                recv_sem=rs_rsem.at[there],
-                device_id={"member": 1 - member, "tensor": t},
-                device_id_type=pl.DeviceIdType.MESH,
-            )
-        )
-        rs_copy[-1].start()
+        pltpu.make_async_remote_copy(
+            src_ref=rs_send.at[here],
+            dst_ref=rs_recv.at[there],
+            send_sem=rs_ssem,
+            recv_sem=rs_rsem,
+            device_id={"member": 1 - member, "tensor": t},
+            device_id_type=pl.DeviceIdType.MESH,
+        ).start()
     for c in side_copy:
         c.wait_recv()
     hidden = res_other[...].astype(f32)
-    for c in rs_copy[::-1]:
-        c.wait_recv()
+    arrival(rs_recv, rs_rsem).wait()
     for i in range(rs_recv.shape[0]):
         hidden = hidden + rs_recv[i].astype(f32)
     ag_ref[...] = (hidden * gain_other[...]).astype(bf16)
-    ag_copy = {}
     for dx, dy in OFFSETS + [(0, 0)]:
         there = slot_of(-dx, -dy)
-        ag_copy[there] = pltpu.make_async_remote_copy(
+        pltpu.make_async_remote_copy(
             src_ref=ag_ref,
             dst_ref=hg_ref.at[there],
-            send_sem=ag_ssem.at[there],
-            recv_sem=ag_rsem.at[there],
+            send_sem=ag_ssem,
+            recv_sem=ag_rsem.at[hops(dx, dy)],
             device_id={"member": 1 - member, "tensor": peer(dx, dy)},
             device_id_type=pl.DeviceIdType.MESH,
-        )
-        ag_copy[there].start()
-
-    for c in w_copy:
-        c.wait()
+        ).start()
+
+    arrival(wh_ref, wh_sem).wait()
     logits, square = 0.0, 0.0
-    nearest = [(0, 0)] + OFFSETS[::-1]
-    for i, (dx, dy) in enumerate(nearest):
-        if i == 0 or hops(dx, dy) != hops(*nearest[i - 1]):
-            for o in nearest:
-                if hops(*o) == hops(dx, dy):
-                    ag_copy[slot_of(*o)].wait_recv()
-        t, k = peer(dx, dy), slot_of(dx, dy)
+    for k, (dx, dy) in enumerate(NEAREST):
+        group = REACH[hops(dx, dy)]
+        if k == group[0]:
+            arrival(hg_ref.at[pl.ds(k, len(group))], ag_rsem.at[hops(dx, dy)]).wait()
+        t = peer(dx, dy)
         here = pl.multiple_of(t * width, width)
         part = hg_ref[k]
         logits = logits + jnp.dot(part, wh_ref[pl.ds(here, width), :], preferred_element_type=f32)
@@ -264,27 +247,23 @@
     stat_ref[0] = jnp.sum(
         jnp.where(lanes // 8 % 8 == subs, spread, f32(0.0)), axis=0, keepdims=True
     )
-    st_copy = []
     for dx, dy in OFFSETS + [(0, 0)]:
         for other in range(2):
             there = slot_of(-dx, -dy) + SIDE * SIDE * other
             if there == 0:
                 continue
-            st_copy.append(
-                pltpu.make_async_remote_copy(
-                    src_ref=stat_ref.at[0],
-                    dst_ref=stat_ref.at[there],
-                    send_sem=st_ssem.at[there - 1],
-                    recv_sem=st_rsem.at[there - 1],
-                    device_id={"member": (member + other) % 2, "tensor": peer(dx, dy)},
-                    device_id_type=pl.DeviceIdType.MESH,
-                )
-            )
-            st_copy[-1].start()
+            pltpu.make_async_remote_copy(
+                src_ref=stat_ref.at[0],
+                dst_ref=stat_ref.at[there],
+                send_sem=st_ssem,
+                recv_sem=st_rsem,
+                device_id={"member": (member + other) % 2, "tensor": peer(dx, dy)},
+                device_id_type=pl.DeviceIdType.MESH,
+            ).start()
     lg_copy.wait_recv()
     mean_logits = 0.5 * (lg_ref[member] + lg_recv[...])
-    for c in st_copy[::-1]:
-        c.wait_recv()
+    got_stats = stat_ref.at[pl.ds(1, stat_ref.shape[0] - 1)]
+    arrival(got_stats, st_rsem).wait()
     log_total, target = 0.0, 0.0
     for other in range(2):
         got = [stat_ref[other * SIDE * SIDE + i] for i in range(SIDE * SIDE)]
@@ -298,7 +277,11 @@
     out_ref[...] = mean_logits - shift
     tout_ref[...] = jnp.broadcast_to(chosen - shift, (half, 128))
 
-    for c in att_copy + side_copy + rs_copy + list(ag_copy.values()) + [lg_copy] + st_copy:
+    arrival(att_recv, att_ssem).wait()
+    arrival(rs_send, rs_ssem).wait()
+    arrival(hg_ref, ag_ssem).wait()
+    arrival(got_stats, st_ssem).wait()
+    for c in side_copy + [lg_copy]:
         c.wait_send()
 
 
@@ -343,12 +326,12 @@
             pltpu.VMEM((2, rows // 2, vocab), f32),
             pltpu.VMEM((rows // 2, vocab), f32),
             pltpu.VMEM((2 * (peers + 1), 1, 128), f32),
-            dma((6,)), dma((2,)), dma((2,)), dma((CHUNKS,)),
-            dma((2,)), dma((2,)), dma((SIDE - 1,)), dma((SIDE - 1,)),
-            dma((peers + 1,)), dma((peers + 1,)),
-            dma((peers + 1,)), dma((peers + 1,)),
+            dma((6,)), dma, dma, dma,
+            dma((2,)), dma((2,)), dma, dma,
             dma, dma,
-            dma((2 * peers + 1,)), dma((2 * peers + 1,)),
+            dma, dma((SIDE + 1,)),
+            dma, dma,
+            dma, dma,
         ],
         compiler_params=pltpu.CompilerParams(
             collective_id=0, has_side_effects=True, vmem_limit_bytes=48 << 20

time: 28.4 us -> 26 us (0.915)
  Pallas kernels: 26.5 us -> 24 us
    pallas_call x1, Pallas kernels: 26.5 us -> 24 us  [local(): pl.pallas_call(step_kernel, out_shape=(jax.ShapeDtypeStruct((rows // 2, v...]
where the time goes in v3:
time: 26 us; the launch traced here: 25.9 us
  Pallas kernels  24 us (92%)
  local copies, waits for them, and re-layouts  1.23 us (5%)
  between operations  0.64 us (2%)
    pallas_call x1, Pallas kernels, local(): pl.pallas_call(step_kernel, out_shape=(jax.ShapeDtypeStruct((rows // 2, v...  24 us
    slice x1, local copies, waits for them, and re-layouts, local(): return (out, target[:, 0])  0.63 us
    unnamed x1, local copies, waits for them, and re-layouts  0.6 us

profile of v3, /device:TPU:1, one launch (start us, length us, event | category | flops | bytes accessed | tf_op | source)
XLA Modules:
  0.0 25.9 jit_solution(2147927182574286839)
XLA Ops:
  0.6 24.0 %decode_step.1 = (f32[4,1024]{1,0:T(4,128)S(1)}, f32[4,128]{1,0:T(4,128)S(1)}) custom-call(bf16[1,8,32,128]{3,2,1,0:T(8,128)(2,1)} %q_hbm.1, bf16[1,8,512,128]{3,2,1,0:T(8,128)(2,1)} %k_hbm.1, bf16[1,8,512,128]{3,2,1,0:T(8,128)(2,1)} %v_hbm.1, s32[8]{0:T(128)} %len_hbm.1, s32[8]{0:T(128)} %tgt_hbm.1, bf16[1,8,4096]{2,1,0:T(8,128)(2,1)} %res_hbm.1, ...), custom_call_target="tpu_custom_call" | custom-call | tf_op jit(solution)/shard_map/decode_step/pallas_call | solution.py:296
  24.6 0.6 %slice_reduce_fusion = f32[4]{0:T(128)} fusion(f32[4,128]{1,0:T(4,128)S(1)} %get-tuple-element.5), kind=kLoop, calls=%fused_computation | loop fusion | bytes 32 | tf_op jit(solution)/shard_map/slice | solution.py:341
  25.3 0.6 %copy.12 = f32[4,1024]{1,0:T(4,128)} copy(f32[4,1024]{1,0:T(4,128)S(1)} %get-tuple-element.8) | data formatting | bytes 32768

commit v4 on v3

--- a/solution.py
+++ b/solution.py
@@ -244,7 +244,7 @@
     lanes = lax.broadcasted_iota(jnp.int32, (rows, 128), 1)
     subs = lax.broadcasted_iota(jnp.int32, (rows, 128), 0)
     spread = jnp.where(lanes < 64, lse, pick)
-    stat_ref[0] = jnp.sum(
+    stat_ref[0:1] = jnp.sum(
         jnp.where(lanes // 8 % 8 == subs, spread, f32(0.0)), axis=0, keepdims=True
     )
     for dx, dy in OFFSETS + [(0, 0)]:
@@ -253,8 +253,8 @@
             if there == 0:
                 continue
             pltpu.make_async_remote_copy(
-                src_ref=stat_ref.at[0],
-                dst_ref=stat_ref.at[there],
+                src_ref=stat_ref.at[0:1],
+                dst_ref=stat_ref.at[there : there + 1],
                 send_sem=st_ssem,
                 recv_sem=st_rsem,
                 device_id={"member": (member + other) % 2, "tensor": peer(dx, dy)},
@@ -266,16 +266,17 @@
     arrival(got_stats, st_rsem).wait()
     log_total, target = 0.0, 0.0
     for other in range(2):
-        got = [stat_ref[other * SIDE * SIDE + i] for i in range(SIDE * SIDE)]
-        peak = functools.reduce(jnp.maximum, got)
-        log_total = log_total + 0.5 * (peak + jnp.log(sum(jnp.exp(g - peak) for g in got)))
-        target = target + 0.5 * sum(got)
+        got = stat_ref[other * SIDE * SIDE : (other + 1) * SIDE * SIDE]
+        peak = jnp.max(got, axis=0, keepdims=True)
+        total = jnp.sum(jnp.exp(got - peak), axis=0, keepdims=True)
+        log_total = log_total + 0.5 * (peak + jnp.log(total))
+        target = target + 0.5 * jnp.sum(got, axis=0, keepdims=True)
     lanes = lax.broadcasted_iota(jnp.int32, (half, 128), 1)
     mine = 8 * (member * half + lax.broadcasted_iota(jnp.int32, (half, 128), 0))
     shift = jnp.sum(jnp.where(lanes == mine, log_total, f32(0.0)), axis=-1, keepdims=True)
     chosen = jnp.sum(jnp.where(lanes == mine + 64, target, f32(0.0)), axis=-1, keepdims=True)
     out_ref[...] = mean_logits - shift
-    tout_ref[...] = jnp.broadcast_to(chosen - shift, (half, 128))
+    tout_ref[...] = (chosen - shift)[:, 0]
 
     arrival(att_recv, att_ssem).wait()
     arrival(rs_send, rs_ssem).wait()
@@ -283,6 +284,17 @@
     arrival(got_stats, st_ssem).wait()
     for c in side_copy + [lg_copy]:
         c.wait_send()
+
+
+def write_out(out_ref, target_ref, out_hbm, target_hbm, out_sem, target_sem):
+    copies = [
+        pltpu.make_async_copy(out_ref, out_hbm, out_sem),
+        pltpu.make_async_copy(target_ref, target_hbm, target_sem),
+    ]
+    for c in copies:
+        c.start()
+    for c in copies:
+        c.wait()
 
 
 def local(queries, keys, values, lengths, targets, residual, out_weight, norm_gain, head_weight):
@@ -297,7 +309,7 @@
         step_kernel,
         out_shape=(
             jax.ShapeDtypeStruct((rows // 2, vocab), f32),
-            jax.ShapeDtypeStruct((rows // 2, 128), f32),
+            jax.ShapeDtypeStruct((rows // 2,), f32),
         ),
         in_specs=[pl.BlockSpec(memory_space=HBM)] * 9,
         out_specs=(
@@ -325,7 +337,7 @@
             pltpu.VMEM((peers + 1, rows, width), bf16),
             pltpu.VMEM((2, rows // 2, vocab), f32),
             pltpu.VMEM((rows // 2, vocab), f32),
-            pltpu.VMEM((2 * (peers + 1), 1, 128), f32),
+            pltpu.VMEM((2 * (peers + 1), 128), f32),
             dma((6,)), dma, dma, dma,
             dma((2,)), dma((2,)), dma, dma,
             dma, dma,
@@ -338,7 +350,18 @@
         ),
         name="decode_step",
     )(*(pltpu.with_memory_space_constraint(a, HBM) for a in (queries, keys, values, lengths, targets, residual, out_weight, norm_gain, head_weight)))
-    return out, target[:, 0]
+    return pl.pallas_call(
+        write_out,
+        out_shape=(
+            jax.ShapeDtypeStruct((rows // 2, vocab), f32),
+            jax.ShapeDtypeStruct((rows // 2,), f32),
+        ),
+        in_specs=[pl.BlockSpec(memory_space=pltpu.MemorySpace.VMEM)] * 2,
+        out_specs=(pl.BlockSpec(memory_space=HBM), pl.BlockSpec(memory_space=HBM)),
+        scratch_shapes=[dma, dma],
+        compiler_params=pltpu.CompilerParams(vmem_limit_bytes=1 << 20),
+        name="write_out",
+    )(out, target)
 
 
 def solution(mesh):

time: 26 us -> 25.3 us (0.973)
  local copies, waits for them, and re-layouts: 1.23 us -> 0 us
  Pallas kernels: 24 us -> 24.6 us
    pallas_call x0 -> x1, Pallas kernels: none -> 0.63 us  [local(): pl.pallas_call(write_out, out_shape=(jax.ShapeDtypeStruct((rows // 2, voc...]
    slice x1 -> x0, local copies, waits for them, and re-layouts: 0.63 us -> none  [local(): return (out, target[:, 0])]
    unnamed x1 -> x0, local copies, waits for them, and re-layouts: 0.6 us -> none
where the time goes in v4:
time: 25.3 us
  Pallas kernels  24.6 us (97%)
  between operations  0.64 us (3%)
    pallas_call x1, Pallas kernels, local(): pl.pallas_call(step_kernel, out_shape=(jax.ShapeDtypeStruct((rows // 2, v...  24 us
    pallas_call x1, Pallas kernels, local(): pl.pallas_call(write_out, out_shape=(jax.ShapeDtypeStruct((rows // 2, voc...  0.63 us

profile of v4, /device:TPU:1, one launch (start us, length us, event | category | flops | bytes accessed | tf_op | source)
XLA Modules:
  0.0 25.3 jit_solution(8400708965430889005)
XLA Ops:
  0.6 24.0 %decode_step.1 = (f32[4,1024]{1,0:T(4,128)S(1)}, f32[4]{0:T(128)S(1)}) custom-call(bf16[1,8,32,128]{3,2,1,0:T(8,128)(2,1)} %q_hbm.1, bf16[1,8,512,128]{3,2,1,0:T(8,128)(2,1)} %k_hbm.1, bf16[1,8,512,128]{3,2,1,0:T(8,128)(2,1)} %v_hbm.1, s32[8]{0:T(128)} %len_hbm.1, s32[8]{0:T(128)} %tgt_hbm.1, bf16[1,8,4096]{2,1,0:T(8,128)(2,1)} %res_hbm.1, ...), custom_call_target="tpu_custom_call" | custom-call | tf_op jit(solution)/shard_map/decode_step/pallas_call | solution.py:308
  24.6 0.6 %write_out.1 = (f32[4,1024]{1,0:T(4,128)}, f32[4]{0:T(128)}) custom-call(f32[4,1024]{1,0:T(4,128)S(1)} %get-tuple-element.4.out_ref, f32[4]{0:T(128)S(1)} %get-tuple-element.5.target_ref), custom_call_target="tpu_custom_call" | custom-call | tf_op jit(solution)/shard_map/write_out/pallas_call | solution.py:353

commit v5 on v4

--- a/solution.py
+++ b/solution.py
@@ -41,7 +41,7 @@
     q_hbm, k_hbm, v_hbm, len_hbm, tgt_hbm, res_hbm, wo_hbm, gain_hbm, wh_hbm,
     out_ref, tout_ref,
     q_ref, k_ref, v_ref, len_ref, tgt_ref, res_ref, wo_ref, gain_ref, inv_ref, wh_ref,
-    res_other, gain_other, att_send, att_recv, rs_send, rs_recv, ag_ref, hg_ref, lg_ref, lg_recv, stat_ref,
+    res_other, gain_mine, gain_other, att_send, att_recv, rs_send, rs_recv, ag_ref, hg_near, hg_mid, lg_ref, lg_recv, stat_ref,
     in_sem, k_sem, v_sem, wh_sem,
     side_ssem, side_rsem, att_ssem, att_rsem, rs_ssem, rs_rsem, ag_ssem, ag_rsem, lg_ssem, lg_rsem, st_ssem, st_rsem,
 ):
@@ -56,15 +56,17 @@
     def peer(dx, dy):
         return (col + dx) % SIDE * SIDE + (row + dy) % SIDE
 
+    def columns(t):
+        return pl.ds(pl.multiple_of(t * width, width), width)
+
     small = [
         pltpu.make_async_copy(q_hbm.at[0, :, pl.ds(col * heads, heads), :], q_ref, in_sem.at[0]),
         pltpu.make_async_copy(len_hbm, len_ref, in_sem.at[1]),
         pltpu.make_async_copy(tgt_hbm, tgt_ref, in_sem.at[2]),
-        pltpu.make_async_copy(
-            res_hbm.at[0, :, pl.ds(pl.multiple_of(me * width, width), width)], res_ref, in_sem.at[3]
-        ),
+        pltpu.make_async_copy(res_hbm.at[0, :, columns(me)], res_ref.at[0], in_sem.at[3]),
         pltpu.make_async_copy(gain_hbm, gain_ref, in_sem.at[4]),
         pltpu.make_async_copy(wo_hbm.at[0], wo_ref, in_sem.at[5]),
+        pltpu.make_async_copy(res_hbm.at[0, :, columns(peer(2, 2))], res_ref.at[1], in_sem.at[6]),
     ]
     half = rows // 2
     k_copy = pltpu.make_async_copy(k_hbm.at[0], k_ref, k_sem)
@@ -135,7 +137,9 @@
         ).start()
     small[3].wait()
     small[4].wait()
-    mine = pl.ds(pl.multiple_of(me * width, width), width)
+    small[6].wait()
+    gain_mine[0] = gain_ref[:, columns(me)]
+    gain_mine[1] = gain_ref[:, columns(peer(2, 2))]
     side_copy = [
         pltpu.make_async_remote_copy(
             src_ref=src,
@@ -145,7 +149,7 @@
             device_id={"member": 1 - member},
             device_id_type=pl.DeviceIdType.MESH,
         )
-        for i, (src, dst) in enumerate([(res_ref, res_other), (gain_ref.at[:, mine], gain_other)])
+        for i, (src, dst) in enumerate([(res_ref, res_other), (gain_mine, gain_other)])
     ]
     for c in side_copy:
         c.start()
@@ -176,18 +180,31 @@
             preferred_element_type=f32,
         )
 
-    for dx, dy in OFFSETS + [(0, 0)]:
-        t = peer(dx, dy)
-        here, there = slot_of(dx, dy), slot_of(-dx, -dy)
-        rs_send[here] = project(t).astype(bf16)
+    def send_pair(dx, dy):
         pltpu.make_async_remote_copy(
-            src_ref=rs_send.at[here],
-            dst_ref=rs_recv.at[there],
+            src_ref=rs_send.at[slot_of(dx, dy)],
+            dst_ref=rs_recv.at[slot_of(-dx, -dy)],
             send_sem=rs_ssem,
             recv_sem=rs_rsem,
-            device_id={"member": 1 - member, "tensor": t},
+            device_id={"member": 1 - member, "tensor": peer(dx, dy)},
             device_id_type=pl.DeviceIdType.MESH,
         ).start()
+
+    later = []
+    for dx, dy in OFFSETS:
+        far, near = (dx, dy), ((dx + 2) % SIDE, (dy + 2) % SIDE)
+        if near in later or far in later:
+            continue
+        far_part = project(peer(*far)).astype(bf16)
+        near_part = project(peer(*near)).astype(bf16)
+        rs_send[slot_of(*far), 0] = far_part
+        rs_send[slot_of(*far), 1] = near_part
+        rs_send[slot_of(*near), 0] = near_part
+        rs_send[slot_of(*near), 1] = far_part
+        send_pair(*far)
+        later.append(near)
+    for near in later:
+        send_pair(*near)
     for c in side_copy:
         c.wait_recv()
     hidden = res_other[...].astype(f32)
@@ -195,29 +212,37 @@
     for i in range(rs_recv.shape[0]):
         hidden = hidden + rs_recv[i].astype(f32)
     ag_ref[...] = (hidden * gain_other[...]).astype(bf16)
+    mid = REACH[2][0]
     for dx, dy in OFFSETS + [(0, 0)]:
-        there = slot_of(-dx, -dy)
+        there, away = slot_of(-dx, -dy), hops(dx, dy)
+        if away > 2:
+            continue
         pltpu.make_async_remote_copy(
-            src_ref=ag_ref,
-            dst_ref=hg_ref.at[there],
-            send_sem=ag_ssem,
-            recv_sem=ag_rsem.at[hops(dx, dy)],
+            src_ref=ag_ref.at[0] if away == 2 else ag_ref,
+            dst_ref=hg_mid.at[there - mid] if away == 2 else hg_near.at[there],
+            send_sem=ag_ssem.at[away // 2],
+            recv_sem=ag_rsem.at[away],
             device_id={"member": 1 - member, "tensor": peer(dx, dy)},
             device_id_type=pl.DeviceIdType.MESH,
         ).start()
 
     arrival(wh_ref, wh_sem).wait()
     logits, square = 0.0, 0.0
-    for k, (dx, dy) in enumerate(NEAREST):
-        group = REACH[hops(dx, dy)]
-        if k == group[0]:
-            arrival(hg_ref.at[pl.ds(k, len(group))], ag_rsem.at[hops(dx, dy)]).wait()
-        t = peer(dx, dy)
-        here = pl.multiple_of(t * width, width)
-        part = hg_ref[k]
-        logits = logits + jnp.dot(part, wh_ref[pl.ds(here, width), :], preferred_element_type=f32)
-        wide = part.astype(f32)
-        square = square + wide * wide * inv_ref[:, pl.ds(here, width)]
+    arrived = [hg_near.at[0:1], hg_near.at[1:mid], hg_mid]
+    for away in range(3):
+        arrival(arrived[away], ag_rsem.at[away]).wait()
+        for k in REACH[away]:
+            dx, dy = NEAREST[k]
+            found = [(peer(dx, dy), hg_mid[k - mid] if away == 2 else hg_near[k, 0])]
+            if away < 2:
+                found.append((peer(dx + 2, dy + 2), hg_near[k, 1]))
+            for t, part in found:
+                here = pl.multiple_of(t * width, width)
+                logits = logits + jnp.dot(
+                    part, wh_ref[pl.ds(here, width), :], preferred_element_type=f32
+                )
+                wide = part.astype(f32)
+                square = square + wide * wide * inv_ref[:, pl.ds(here, width)]
     mean_square = jnp.sum(square, axis=-1, keepdims=True) * (1.0 / model)
     logits = logits * lax.rsqrt(mean_square + 1e-05)
     lg_ref[0] = logits[:half]
@@ -280,7 +305,8 @@
 
     arrival(att_recv, att_ssem).wait()
     arrival(rs_send, rs_ssem).wait()
-    arrival(hg_ref, ag_ssem).wait()
+    arrival(hg_near, ag_ssem.at[0]).wait()
+    arrival(hg_mid, ag_ssem.at[1]).wait()
     arrival(got_stats, st_ssem).wait()
     for c in side_copy + [lg_copy]:
         c.wait_send()
@@ -322,26 +348,28 @@
             pltpu.VMEM((rows, span, depth), bf16),
             pltpu.SMEM((rows,), jnp.int32),
             pltpu.SMEM((rows,), jnp.int32),
-            pltpu.VMEM((rows, width), bf16),
+            pltpu.VMEM((2, rows, width), bf16),
             pltpu.VMEM((width, model), bf16),
             pltpu.VMEM((1, model), f32),
             pltpu.VMEM((1, model), f32),
             pltpu.VMEM((model, vocab), bf16),
-            pltpu.VMEM((rows, width), bf16),
-            pltpu.VMEM((1, width), f32),
+            pltpu.VMEM((2, rows, width), bf16),
+            pltpu.VMEM((2, 1, width), f32),
+            pltpu.VMEM((2, 1, width), f32),
             pltpu.VMEM((2 * heads * rows, depth), f32),
             pltpu.VMEM((SIDE - 1, 4 * rows, depth), f32),
-            pltpu.VMEM((peers + 1, rows, width), bf16),
-            pltpu.VMEM((peers + 1, rows, width), bf16),
-            pltpu.VMEM((rows, width), bf16),
-            pltpu.VMEM((peers + 1, rows, width), bf16),
+            pltpu.VMEM((peers + 1, 2, rows, width), bf16),
+            pltpu.VMEM((peers + 1, 2, rows, width), bf16),
+            pltpu.VMEM((2, rows, width), bf16),
+            pltpu.VMEM((len(REACH[0] + REACH[1]), 2, rows, width), bf16),
+            pltpu.VMEM((len(REACH[2]), rows, width), bf16),
             pltpu.VMEM((2, rows // 2, vocab), f32),
             pltpu.VMEM((rows // 2, vocab), f32),
             pltpu.VMEM((2 * (peers + 1), 128), f32),
-            dma((6,)), dma, dma, dma,
+            dma((7,)), dma, dma, dma,
             dma((2,)), dma((2,)), dma, dma,
             dma, dma,
-            dma, dma((SIDE + 1,)),
+            dma((2,)), dma((3,)),
             dma, dma,
             dma, dma,
         ],

time: 25.3 us -> 24.6 us (0.972)
  Pallas kernels: 24.6 us -> 23.9 us
    pallas_call x1, Pallas kernels: 24 us -> 23.3 us  [local(): pl.pallas_call(step_kernel, out_shape=(jax.ShapeDtypeStruct((rows // 2, v...]
where the time goes in v5:
time: 24.6 us
  Pallas kernels  23.9 us (97%)
  between operations  0.64 us (3%)
    pallas_call x1, Pallas kernels, local(): pl.pallas_call(step_kernel, out_shape=(jax.ShapeDtypeStruct((rows // 2, v...  23.3 us
    pallas_call x1, Pallas kernels, local(): pl.pallas_call(write_out, out_shape=(jax.ShapeDtypeStruct((rows // 2, voc...  0.63 us

profile of v5, /device:TPU:1, one launch (start us, length us, event | category | flops | bytes accessed | tf_op | source)
XLA Modules:
  0.0 24.6 jit_solution(2473957979295834238)
XLA Ops:
  0.6 23.3 %decode_step.1 = (f32[4,1024]{1,0:T(4,128)S(1)}, f32[4]{0:T(128)S(1)}) custom-call(bf16[1,8,32,128]{3,2,1,0:T(8,128)(2,1)} %q_hbm.1, bf16[1,8,512,128]{3,2,1,0:T(8,128)(2,1)} %k_hbm.1, bf16[1,8,512,128]{3,2,1,0:T(8,128)(2,1)} %v_hbm.1, s32[8]{0:T(128)} %len_hbm.1, s32[8]{0:T(128)} %tgt_hbm.1, bf16[1,8,4096]{2,1,0:T(8,128)(2,1)} %res_hbm.1, ...), custom_call_target="tpu_custom_call" | custom-call | tf_op jit(solution)/shard_map/decode_step/pallas_call | solution.py:334
  23.9 0.6 %write_out.1 = (f32[4,1024]{1,0:T(4,128)}, f32[4]{0:T(128)}) custom-call(f32[4,1024]{1,0:T(4,128)S(1)} %get-tuple-element.4.out_ref, f32[4]{0:T(128)S(1)} %get-tuple-element.5.target_ref), custom_call_target="tpu_custom_call" | custom-call | tf_op jit(solution)/shard_map/write_out/pallas_call | solution.py:381

commit v6 on v5

--- a/solution.py
+++ b/solution.py
@@ -27,6 +27,9 @@
 NEAREST = [(0, 0)] + OFFSETS[::-1]
 SLOT = {o: i for i, o in enumerate(NEAREST)}
 REACH = [[i for i, o in enumerate(NEAREST) if hops(*o) == n] for n in range(SIDE + 1)]
+
+
+HALF_MID = len(REACH[2]) // 2
 
 
 def slot_of(dx, dy):
@@ -54,7 +57,7 @@
     f32, bf16 = jnp.float32, jnp.bfloat16
 
     def peer(dx, dy):
-        return (col + dx) % SIDE * SIDE + (row + dy) % SIDE
+        return (col + dx % SIDE) % SIDE * SIDE + (row + dy % SIDE) % SIDE
 
     def columns(t):
         return pl.ds(pl.multiple_of(t * width, width), width)
@@ -203,7 +206,7 @@
         rs_send[slot_of(*near), 1] = far_part
         send_pair(*far)
         later.append(near)
-    for near in later:
+    for near in sorted(later, key=lambda o: -hops(*o)):
         send_pair(*near)
     for c in side_copy:
         c.wait_recv()
@@ -212,30 +215,35 @@
     for i in range(rs_recv.shape[0]):
         hidden = hidden + rs_recv[i].astype(f32)
     ag_ref[...] = (hidden * gain_other[...]).astype(bf16)
-    mid = REACH[2][0]
+    mids = [o for o in OFFSETS if hops(*o) == 2]
     for dx, dy in OFFSETS + [(0, 0)]:
         there, away = slot_of(-dx, -dy), hops(dx, dy)
+        order = mids.index((dx, dy)) if away == 2 else 0
         if away > 2:
             continue
         pltpu.make_async_remote_copy(
             src_ref=ag_ref.at[0] if away == 2 else ag_ref,
-            dst_ref=hg_mid.at[there - mid] if away == 2 else hg_near.at[there],
+            dst_ref=hg_mid.at[order] if away == 2 else hg_near.at[there],
             send_sem=ag_ssem.at[away // 2],
-            recv_sem=ag_rsem.at[away],
+            recv_sem=ag_rsem.at[away + order // HALF_MID],
             device_id={"member": 1 - member, "tensor": peer(dx, dy)},
             device_id_type=pl.DeviceIdType.MESH,
         ).start()
 
     arrival(wh_ref, wh_sem).wait()
     logits, square = 0.0, 0.0
-    arrived = [hg_near.at[0:1], hg_near.at[1:mid], hg_mid]
-    for away in range(3):
-        arrival(arrived[away], ag_rsem.at[away]).wait()
-        for k in REACH[away]:
-            dx, dy = NEAREST[k]
-            found = [(peer(dx, dy), hg_mid[k - mid] if away == 2 else hg_near[k, 0])]
+    near = len(REACH[0] + REACH[1])
+    groups = [(hg_near.at[0:1], range(1)), (hg_near.at[1:near], range(1, near))]
+    for i in range(0, len(mids), HALF_MID):
+        groups.append((hg_mid.at[i : i + HALF_MID], mids[i : i + HALF_MID]))
+    for away, (arrived, sources) in enumerate(groups):
+        arrival(arrived, ag_rsem.at[away]).wait()
+        for k in sources:
             if away < 2:
-                found.append((peer(dx + 2, dy + 2), hg_near[k, 1]))
+                dx, dy = NEAREST[k]
+                found = [(peer(dx, dy), hg_near[k, 0]), (peer(dx + 2, dy + 2), hg_near[k, 1])]
+            else:
+                found = [(peer(-k[0], -k[1]), hg_mid[mids.index(k)])]
             for t, part in found:
                 here = pl.multiple_of(t * width, width)
                 logits = logits + jnp.dot(
@@ -273,7 +281,7 @@
         jnp.where(lanes // 8 % 8 == subs, spread, f32(0.0)), axis=0, keepdims=True
     )
     for dx, dy in OFFSETS + [(0, 0)]:
-        for other in range(2):
+        for other in (1, 0):
             there = slot_of(-dx, -dy) + SIDE * SIDE * other
             if there == 0:
                 continue
@@ -369,7 +377,7 @@
             dma((7,)), dma, dma, dma,
             dma((2,)), dma((2,)), dma, dma,
             dma, dma,
-            dma((2,)), dma((3,)),
+            dma((2,)), dma((2 + len(REACH[2]) // HALF_MID,)),
             dma, dma,
             dma, dma,
         ],

time: 24.6 us -> 24.5 us (level)
  no operation moved by 1% of the time
where the time goes in v6:
time: 24.5 us; the launch traced here: 24.4 us
  Pallas kernels  23.7 us (97%)
  between operations  0.64 us (3%)
    pallas_call x1, Pallas kernels, local(): pl.pallas_call(step_kernel, out_shape=(jax.ShapeDtypeStruct((rows // 2, v...  23.1 us
    pallas_call x1, Pallas kernels, local(): pl.pallas_call(write_out, out_shape=(jax.ShapeDtypeStruct((rows // 2, voc...  0.63 us

profile of v6, /device:TPU:1, one launch (start us, length us, event | category | flops | bytes accessed | tf_op | source)
XLA Modules:
  0.0 24.4 jit_solution(13595050110427946314)
XLA Ops:
  0.6 23.1 %decode_step.1 = (f32[4,1024]{1,0:T(4,128)S(1)}, f32[4]{0:T(128)S(1)}) custom-call(bf16[1,8,32,128]{3,2,1,0:T(8,128)(2,1)} %q_hbm.1, bf16[1,8,512,128]{3,2,1,0:T(8,128)(2,1)} %k_hbm.1, bf16[1,8,512,128]{3,2,1,0:T(8,128)(2,1)} %v_hbm.1, s32[8]{0:T(128)} %len_hbm.1, s32[8]{0:T(128)} %tgt_hbm.1, bf16[1,8,4096]{2,1,0:T(8,128)(2,1)} %res_hbm.1, ...), custom_call_target="tpu_custom_call" | custom-call | tf_op jit(solution)/shard_map/decode_step/pallas_call | solution.py:342
  23.7 0.6 %write_out.1 = (f32[4,1024]{1,0:T(4,128)}, f32[4]{0:T(128)}) custom-call(f32[4,1024]{1,0:T(4,128)S(1)} %get-tuple-element.4.out_ref, f32[4]{0:T(128)S(1)} %get-tuple-element.5.target_ref), custom_call_target="tpu_custom_call" | custom-call | tf_op jit(solution)/shard_map/write_out/pallas_call | solution.py:389

commit v7 on v5

--- a/solution.py
+++ b/solution.py
@@ -83,6 +83,9 @@
     small[1].start()
     k_copy.start()
     v_copy.start()
+    for c in small[2:] + w_copy:
+        c.start()
+
     barrier = pltpu.get_barrier_semaphore()
     near = [o for o in OFFSETS + [(0, 0)] if 0 in o]
     for dx, dy in near:
@@ -95,8 +98,6 @@
                 device_id={"member": (member + other) % 2, "tensor": peer(dx, dy)},
                 device_id_type=pl.DeviceIdType.MESH,
             )
-    for c in small[2:] + w_copy:
-        c.start()
 
     small[0].wait()
     small[1].wait()

time: 24.6 us -> 27 us (1.098)
  Pallas kernels: 23.9 us -> 26.3 us
    pallas_call x1, Pallas kernels: 23.3 us -> 25.6 us  [local(): pl.pallas_call(step_kernel, out_shape=(jax.ShapeDtypeStruct((rows // 2, v...]
where the time goes in v7:
time: 27 us; the launch traced here: 26.9 us
  Pallas kernels  26.3 us (97%)
  between operations  0.64 us (2%)
    pallas_call x1, Pallas kernels, local(): pl.pallas_call(step_kernel, out_shape=(jax.ShapeDtypeStruct((rows // 2, v...  25.6 us
    pallas_call x1, Pallas kernels, local(): pl.pallas_call(write_out, out_shape=(jax.ShapeDtypeStruct((rows // 2, voc...  0.63 us

profile of v7, /device:TPU:1, one launch (start us, length us, event | category | flops | bytes accessed | tf_op | source)
XLA Modules:
  0.0 26.9 jit_solution(16226776121772233325)
XLA Ops:
  0.6 25.6 %decode_step.1 = (f32[4,1024]{1,0:T(4,128)S(1)}, f32[4]{0:T(128)S(1)}) custom-call(bf16[1,8,32,128]{3,2,1,0:T(8,128)(2,1)} %q_hbm.1, bf16[1,8,512,128]{3,2,1,0:T(8,128)(2,1)} %k_hbm.1, bf16[1,8,512,128]{3,2,1,0:T(8,128)(2,1)} %v_hbm.1, s32[8]{0:T(128)} %len_hbm.1, s32[8]{0:T(128)} %tgt_hbm.1, bf16[1,8,4096]{2,1,0:T(8,128)(2,1)} %res_hbm.1, ...), custom_call_target="tpu_custom_call" | custom-call | tf_op jit(solution)/shard_map/decode_step/pallas_call | solution.py:335
  26.3 0.6 %write_out.1 = (f32[4,1024]{1,0:T(4,128)}, f32[4]{0:T(128)}) custom-call(f32[4,1024]{1,0:T(4,128)S(1)} %get-tuple-element.4.out_ref, f32[4]{0:T(128)S(1)} %get-tuple-element.5.target_ref), custom_call_target="tpu_custom_call" | custom-call | tf_op jit(solution)/shard_map/write_out/pallas_call | solution.py:382
